TPU v7x, 256 devices: a whole 4x4x8 slice. The times are simulated.
256 devices in a mesh: rep: 16 (over x_hi, z), head: 8 (over y, core), pair: 2 (over x_lo).
Axes of the slice: x: 4 (x_hi: 2, x_lo: 2; x = x_hi * 2 + x_lo), y: 4, z: 8, core: 2. Of those that a mesh axis runs over, the one named last changes fastest.
Arguments:
- queries: bfloat16 [384, 8192], P(('rep', 'pair'), 'head'), may hold values from -24 to 24
- new_keys: bfloat16 [384, 1024], P(('rep', 'pair'), 'head'), may hold values from -6 to 6
- new_values: bfloat16 [384, 1024], P(('rep', 'pair'), 'head'), may hold values from -6 to 6
- key_cache: bfloat16 [384, 1024, 1024], P(('rep', 'pair'), None, 'head'), may hold values from -6 to 6
- value_cache: bfloat16 [384, 1024, 1024], P(('rep', 'pair'), None, 'head'), may hold values from -6 to 6
- lengths: int32 [384], P(('rep', 'pair')), may hold values from 2 to 1024
- residual: bfloat16 [384, 8192], P('head', ('rep', 'pair')), may hold values from -36 to 36
- norm_gain: float32 [8192], replicated, may hold values from 0.5 to 1.5
- out_weight: bfloat16 [8192, 8192], P('head', ('rep', 'pair')), may hold values from -0.5 to 0.5
- gate_weight: bfloat16 [8192, 28672], P('head', ('rep', 'pair')), may hold values from -0.0625 to 0.0625
- up_weight: bfloat16 [8192, 28672], P('head', ('rep', 'pair')), may hold values from -0.0625 to 0.0625
- down_weight: bfloat16 [28672, 8192], P(('rep', 'pair'), 'head'), may hold values from -0.03125 to 0.03125
Outputs:
- hidden_state: bfloat16 [384, 8192], P('head', ('rep', 'pair'))
- ffn_out: bfloat16 [384, 8192], P(('rep', 'pair'), 'head')
Inputs may be any that keep to these rules, and one draw needn't show every extreme that they name: Cache slots 0 to lengths - 1 of a row are live, the others are ignored.
All inputs are finite; a program needn't handle non-finite values.
Results may differ from a plain program's by a relative error of at most 0.0095.
Values may be sent and summed in bfloat16 or wider, within the bound.
No kernel may reach another device: no remote copies, remote signals or barrier semaphores. Data moves between devices by JAX's collectives and lax.ppermute only.
A program may use at most 64 MiB of HBM per device.

v0:
```python
import jax
import jax.numpy as jnp
from jax import lax
from jax.sharding import PartitionSpec as P

HEADS = 64
KV_HEADS = 8
HEAD_DIM = 128


def sent_to_all(array, axis):
    copies = jnp.broadcast_to(array, (lax.axis_size(axis), *array.shape))
    return lax.all_to_all(copies, axis, split_axis=0, concat_axis=0, tiled=True)


def in_order(pieces, dim):
    dims = list(pieces.shape[1:])
    dims[dim] *= pieces.shape[0]
    return jnp.moveaxis(pieces, 0, dim).reshape(dims)


def gathered_copies(array, axis, dim):
    pieces = sent_to_all(array, axis)
    return in_order(pieces, dim)


def cut_along(array, dim, size):
    dims = array.shape
    pieces = array.reshape(*dims[:dim], size, dims[dim] // size, *dims[dim + 1 :])
    return jnp.moveaxis(pieces, dim, 0)


def sent_and_summed(array, axis, dim):
    size = lax.axis_size(axis)
    pieces = lax.all_to_all(cut_along(array, dim, size), axis, 0, 0, tiled=True)
    return jnp.sum(pieces, axis=0)


def side_by_side(arrays, axis, dim, along):
    both = jnp.concatenate(arrays, axis=along)
    filled, at, done = (sent_and_summed(both, axis, dim), 0, [])
    for a in arrays:
        done.append(lax.slice_in_dim(filled, at, at + a.shape[along], axis=along))
        at += a.shape[along]
    return tuple(done)


def local(
    queries,
    new_keys,
    new_values,
    key_cache,
    value_cache,
    lengths,
    residual,
    norm_gain,
    out_weight,
    gate_weight,
    up_weight,
    down_weight,
):
    row_count = queries.shape[0]
    slot_count = key_cache.shape[1]
    kv_local = key_cache.shape[2] // HEAD_DIM
    group_size = HEADS // KV_HEADS
    score_scale = HEAD_DIM ** (-0.5)
    query_heads = queries.reshape(row_count, kv_local, group_size, HEAD_DIM)
    cached_keys = key_cache.reshape(row_count, slot_count, kv_local, HEAD_DIM)
    cached_values = value_cache.reshape(row_count, slot_count, kv_local, HEAD_DIM)
    key_new = new_keys.reshape(row_count, kv_local, HEAD_DIM)
    value_new = new_values.reshape(row_count, kv_local, HEAD_DIM).astype(jnp.float32)
    scores = (
        jnp.einsum("rhgd,rchd->rhgc", query_heads, cached_keys, preferred_element_type=jnp.float32)
        * score_scale
    )
    slot_ids = lax.broadcasted_iota(jnp.int32, (row_count, 1, 1, slot_count), 3)
    live_mask = slot_ids < lengths[:, None, None, None]
    scores = jnp.where(live_mask, scores, -jnp.inf)
    own_score = (
        jnp.einsum("rhgd,rhd->rhg", query_heads, key_new, preferred_element_type=jnp.float32)
        * score_scale
    )
    row_top = jnp.maximum(jnp.max(scores, axis=3), own_score)
    weights = jnp.exp(scores - row_top[..., None])
    own_weight = jnp.exp(own_score - row_top)
    weight_total = jnp.sum(weights, axis=3) + own_weight
    weights_low = weights.astype(jnp.bfloat16)
    own_low = own_weight.astype(jnp.bfloat16).astype(jnp.float32)
    mixture = jnp.einsum(
        "rhgc,rchd->rhgd", weights_low, cached_values, preferred_element_type=jnp.float32
    )
    mixture = mixture + own_low[..., None] * value_new[:, :, None, :]
    attn = (mixture / weight_total[..., None]).astype(jnp.bfloat16).reshape(row_count, -1)
    projected_terms = jnp.dot(
        gathered_copies(attn, ("rep", "pair"), 0), out_weight, preferred_element_type=jnp.float32
    )
    projected = sent_and_summed(projected_terms, "head", 0)
    hidden_state = (residual.astype(jnp.float32) + projected).astype(jnp.bfloat16)
    full_rows = gathered_copies(hidden_state, ("rep", "pair"), 1)
    state_f = full_rows.astype(jnp.float32)
    mean_square = jnp.mean(state_f * state_f, axis=1, keepdims=True)
    normed = (state_f * lax.rsqrt(mean_square + 1e-05) * norm_gain).astype(jnp.bfloat16)
    normed_cols = lax.all_to_all(normed, "head", split_axis=1, concat_axis=0, tiled=True)
    gate_part = jnp.dot(normed_cols, gate_weight, preferred_element_type=jnp.float32)
    up_part = jnp.dot(normed_cols, up_weight, preferred_element_type=jnp.float32)
    gate_share, up_share = side_by_side((gate_part, up_part), "head", 1, 0)
    hidden_share = (jax.nn.silu(gate_share) * up_share).astype(jnp.bfloat16)
    hidden = gathered_copies(hidden_share, "head", 1)
    ffn_out = sent_and_summed(
        jnp.dot(hidden, down_weight, preferred_element_type=jnp.float32), ("rep", "pair"), 0
    )
    return (hidden_state, ffn_out.astype(jnp.bfloat16))


def solution(mesh):
    placed = (
        P(("rep", "pair"), "head"),
        P(("rep", "pair"), "head"),
        P(("rep", "pair"), "head"),
        P(("rep", "pair"), None, "head"),
        P(("rep", "pair"), None, "head"),
        P(("rep", "pair")),
        P("head", ("rep", "pair")),
        P(),
        P("head", ("rep", "pair")),
        P("head", ("rep", "pair")),
        P("head", ("rep", "pair")),
        P(("rep", "pair"), "head"),
    )
    return jax.shard_map(
        local,
        mesh=mesh,
        in_specs=placed,
        out_specs=(P("head", ("rep", "pair")), P(("rep", "pair"), "head")),
        check_vma=False,
    )
```

profile of v0, /device:TPU:32, one launch (start us, length us, event | category | flops | bytes accessed | tf_op | source)
XLA Modules:
  0.0 252.3 jit_solution(8546242657127766554)
XLA Ops:
  0.6 0.0 copy-start
  0.6 0.8 convert_element_type.54
  1.5 0.8 iota_compare_fusion
  2.3 0.8 copy.25
  3.1 0.8 fusion.14
  3.9 0.0 copy-done
  3.9 0.0 copy-start.1
  3.9 1.0 fusion.22
  4.9 0.2 fusion.9
  5.2 0.6 copy-done.1
  5.8 0.6 fusion.5
  6.4 0.1 broadcast_in_dim.30
  6.5 40.7 %all_to_all.46 = bf16[32,12,1024]{2,1,0:T(8,128)(2,1)} all-to-all(bf16[32,12,1024]{2,1,0:T(8,128)(2,1)S(1)} %broadcast_in_dim.30), channel_id=1, replica_groups=mesh['rep'=16,'head'=8,'pair'=2] {'rep','pair'}, dimensions={0} | all-to-all | bytes 1572864 | tf_op jit(solution)/shard_map/all_to_all | solution.py:13
  47.3 2.1 dot_general.28
  49.4 1.6 fusion.7
  51.0 13.2 %all_to_all.47 = f32[8,48,256]{2,1,0:T(8,128)S(1)} all-to-all(f32[8,48,256]{2,1,0:T(8,128)S(1)} %fusion.7), channel_id=1, replica_groups=mesh['rep'=16,'head'=8,'pair'=2] {'head'}, dimensions={0} | all-to-all | bytes 786432 | tf_op jit(solution)/shard_map/all_to_all | solution.py:35
  64.3 0.6 reduce_sum.46
  64.9 0.8 add_convert_fusion
  65.7 1.0 broadcast_in_dim.31
  66.7 4.7 %all-to-all-start.2 = ((bf16[32,48,256]{2,1,0:T(8,128)(2,1)}), bf16[32,48,256]{2,1,0:T(8,128)(2,1)}, u32[]{:S(2)}, u32[]{:S(2)}) async-start(bf16[32,48,256]{2,1,0:T(8,128)(2,1)} %broadcast_in_dim.31), calls=%async_computation.2 | async-start | bytes 1572864 | tf_op jit(solution)/shard_map/all_to_all | solution.py:13
  71.4 0.0 copy-done.3
  71.4 24.2 %all-to-all-done.2 = bf16[32,48,256]{2,1,0:T(8,128)(2,1)} async-done(((bf16[32,48,256]{2,1,0:T(8,128)(2,1)}), bf16[32,48,256]{2,1,0:T(8,128)(2,1)}, u32[]{:S(2)}, u32[]{:S(2)}) %all-to-all-start.2) | async-done | bytes 786464 | tf_op jit(solution)/shard_map/all_to_all | solution.py:13
  95.6 1.4 fusion.2
  97.0 1.3 convert_bitcast_fusion
  98.4 0.0 copy-done.2
  98.4 2.1 copy.17
  100.5 2.7 %reshape.129 = f32[48,8,1024]{2,1,0:T(8,128)} reshape(f32[48,32,256]{2,1,0:T(8,128)} %copy.17) | data formatting | bytes 3145728 | tf_op jit(solution)/shard_map/convert_element_type | solution.py:100
  103.1 1.6 multiply_convert_fusion
  104.7 0.0 copy-start.4
  104.7 0.4 copy.18
  105.2 15.8 %all_to_all.48 = bf16[48,8,1024]{2,0,1:T(8,128)(2,1)S(1)} all-to-all(bf16[48,8,1024]{2,0,1:T(8,128)(2,1)S(1)} %copy.18), channel_id=1, replica_groups=mesh['rep'=16,'head'=8,'pair'=2] {'head'}, dimensions={1} | all-to-all | bytes 1572864 | tf_op jit(solution)/shard_map/all_to_all | solution.py:103
  121.0 0.0 copy-done.4
  121.0 1.0 fusion.24
  122.0 0.5 copy-done.5
  122.5 1.0 fusion.23
  123.5 1.7 pad_maximum_fusion
  125.2 3.4 %copy.19 = f32[768,896]{0,1:T(8,128)} copy(f32[768,896]{1,0:T(8,128)} %pad_maximum_fusion) | data formatting | bytes 5505024 | tf_op jit(solution)/shard_map/concatenate | solution.py:40
  128.6 39.0 %all_to_all.49 = f32[8,768,112]{1,2,0:T(8,128)} all-to-all(f32[8,768,112]{1,2,0:T(8,128)} %bitcast.45), channel_id=1, replica_groups=mesh['rep'=16,'head'=8,'pair'=2] {'head'}, dimensions={0} | all-to-all | bytes 5505024 | tf_op jit(solution)/shard_map/all_to_all | solution.py:35
  167.6 2.0 reduce_sum.48
  169.6 0.1 fusion.13
  169.6 0.1 broadcast_in_dim.32
  169.7 15.2 %all_to_all.50 = bf16[8,384,112]{1,2,0:T(8,128)(2,1)} all-to-all(bf16[8,384,112]{1,2,0:T(8,128)(2,1)S(1)} %broadcast_in_dim.32), channel_id=1, replica_groups=mesh['rep'=16,'head'=8,'pair'=2] {'head'}, dimensions={0} | all-to-all | bytes 1376256 | tf_op jit(solution)/shard_map/all_to_all | solution.py:13
  184.9 2.4 copy.20
  187.4 2.6 %dot_general.32 = bf16[32,12,896]{2,1,0:T(8,128)(2,1)} reshape(bf16[384,8,112]{2,1,0:T(8,128)(2,1)} %copy.20) | data formatting | bytes 1376256 | tf_op jit(solution)/shard_map/dot_general | solution.py:110
  190.0 2.8 %fusion = f32[32,12,1024]{2,0,1:T(8,128)S(1)} fusion(bf16[896,1024]{1,0:T(8,128)(2,1)} %param.23, bf16[32,12,896]{2,1,0:T(8,128)(2,1)} %dot_general.32), kind=kOutput, calls=%fused_computation.3 | convolution fusion | flops 704643072 | bytes 4096000 | tf_op jit(solution)/shard_map/dot_general | solution.py:110
  192.8 0.9 copy.22
  193.7 56.3 %all_to_all.51 = f32[32,12,1024]{2,1,0:T(8,128)} all-to-all(f32[32,12,1024]{2,1,0:T(8,128)S(1)} %copy.22), channel_id=1, replica_groups=mesh['rep'=16,'head'=8,'pair'=2] {'rep','pair'}, dimensions={0} | all-to-all | bytes 3145728 | tf_op jit(solution)/shard_map/all_to_all | solution.py:35
  250.0 2.3 reduce_sum.49
  (9 shorter events, 0.1 us)
Async XLA Ops:
  0.6 3.3 %copy-start = (bf16[12,1024,128]{2,1,0:T(8,128)(2,1)S(1)}, bf16[12,1024,128]{2,1,0:T(8,128)(2,1)}, u32[]{:S(2)}) copy-start(bf16[12,1024,128]{2,1,0:T(8,128)(2,1)} %param.15) | copy-start | bytes 9437188
  3.9 1.9 copy-start.1
  64.9 6.5 %copy-start.3 = (f32[8192]{0:T(1024)S(1)}, f32[8192]{0:T(1024)}, u32[]{:S(2)}) copy-start(f32[8192]{0:T(1024)} %param.19) | copy-start | bytes 98308
  65.7 32.7 %copy-start.2 = (bf16[48,256]{1,0:T(8,128)(2,1)}, bf16[48,256]{1,0:T(8,128)(2,1)S(1)}, u32[]{:S(2)}) copy-start(bf16[48,256]{1,0:T(8,128)(2,1)S(1)} %add_convert_fusion) | copy-start | bytes 73732
  66.7 29.0 %all-to-all-start.2 = ((bf16[32,48,256]{2,1,0:T(8,128)(2,1)}), bf16[32,48,256]{2,1,0:T(8,128)(2,1)}, u32[]{:S(2)}, u32[]{:S(2)}) async-start(bf16[32,48,256]{2,1,0:T(8,128)(2,1)} %broadcast_in_dim.31), calls=%async_computation.2 | async-start | bytes 1572864 | tf_op jit(solution)/shard_map/all_to_all | solution.py:13
  104.7 16.3 %copy-start.4 = (bf16[1024,896]{1,0:T(8,128)(2,1)S(1)}, bf16[1024,896]{1,0:T(8,128)(2,1)}, u32[]{:S(2)}) copy-start(bf16[1024,896]{1,0:T(8,128)(2,1)} %param.22) | copy-start | bytes 5505028
  121.0 1.5 copy-start.5
where the time goes:
time: 253 us; the launch traced here: 252 us
  blocking collectives  180 us (71%)
  waiting for transfers between devices  24.2 us (10%)
  local copies, waits for them, and re-layouts  19.8 us (8%)
  other arithmetic  13.8 us (5%)
  matrix products  8.74 us (3%)
  starting transfers between devices  4.69 us (2%)
    all_to_all x3, blocking collectives, sent_and_summed(): pieces = lax.all_to_all(cut_along(array, dim, size), axis, 0, 0, tiled=True)  108 us
    all_to_all x2, blocking collectives, sent_to_all(): return lax.all_to_all(copies, axis, split_axis=0, concat_axis=0, tiled=True)  55.9 us
    all_to_all x1, waiting for transfers between devices, sent_to_all(): return lax.all_to_all(copies, axis, split_axis=0, concat_axis=0, tiled=True)  24.2 us
    all_to_all x1, blocking collectives, local(): lax.all_to_all(normed, 'head', split_axis=1, concat_axis=0, tiled=True)  15.8 us
  transfers between devices with their start and end apart: 1, of which 1 were waited for; matrix products, arithmetic and copies ran while one was open for 0% of the time, Pallas kernels for 0%

commit v1 on v0

--- a/solution.py
+++ b/solution.py
@@ -100,7 +100,10 @@
     state_f = full_rows.astype(jnp.float32)
     mean_square = jnp.mean(state_f * state_f, axis=1, keepdims=True)
     normed = (state_f * lax.rsqrt(mean_square + 1e-05) * norm_gain).astype(jnp.bfloat16)
-    normed_cols = lax.all_to_all(normed, "head", split_axis=1, concat_axis=0, tiled=True)
+    normed_cols = jnp.concatenate(
+        lax.all_to_all(jnp.stack(jnp.split(normed, lax.axis_size("head"), axis=1)), "head", 0, 0),
+        axis=0,
+    )
     gate_part = jnp.dot(normed_cols, gate_weight, preferred_element_type=jnp.float32)
     up_part = jnp.dot(normed_cols, up_weight, preferred_element_type=jnp.float32)
     gate_share, up_share = side_by_side((gate_part, up_part), "head", 1, 0)

time: 253 us -> 243 us (0.960)
  blocking collectives: 180 us -> 208 us
  waiting for transfers between devices: 24.2 us -> 0 us
  local copies, waits for them, and re-layouts: 19.8 us -> 14.5 us
  starting transfers between devices: 4.69 us -> 0 us
  other arithmetic: 13.8 us -> 10.1 us
    all_to_all x2 -> x3, blocking collectives: 55.9 us -> 83.6 us  [sent_to_all(): return lax.all_to_all(copies, axis, split_axis=0, concat_axis=0, tiled=True)]
    all_to_all x1 -> x0, waiting for transfers between devices: 24.2 us -> none  [sent_to_all(): return lax.all_to_all(copies, axis, split_axis=0, concat_axis=0, tiled=True)]
    all_to_all x1 -> x0, starting transfers between devices: 4.69 us -> none  [sent_to_all(): return lax.all_to_all(copies, axis, split_axis=0, concat_axis=0, tiled=True)]
    convert_element_type x2 -> x1, local copies, waits for them, and re-layouts: 4.74 us -> 0.13 us  [local(): state_f = full_rows.astype(jnp.float32)]
  transfers between devices with their start and end apart: 1 -> 0, of which waited for: 1 -> 0; matrix products, arithmetic and copies ran while one was open for 0% -> 0% of each run, Pallas kernels for 0% -> 0%
where the time goes in v1:
time: 243 us; the launch traced here: 242 us
  blocking collectives  208 us (86%)
  local copies, waits for them, and re-layouts  14.5 us (6%)
  other arithmetic  10.1 us (4%)
  matrix products  8.72 us (4%)
    all_to_all x3, blocking collectives, sent_and_summed(): pieces = lax.all_to_all(cut_along(array, dim, size), axis, 0, 0, tiled=True)  108 us
    all_to_all x3, blocking collectives, sent_to_all(): return lax.all_to_all(copies, axis, split_axis=0, concat_axis=0, tiled=True)  83.6 us
    all_to_all x1, blocking collectives, local(): lax.all_to_all(jnp.stack(jnp.split(normed, lax.axis_size('head'), axis=1)...  15.8 us
    reduce_sum x3, other arithmetic, sent_and_summed(): return jnp.sum(pieces, axis=0)  4.94 us

profile of v1, /device:TPU:32, one launch (start us, length us, event | category | flops | bytes accessed | tf_op | source)
XLA Modules:
  0.0 242.2 jit_solution(3939100175109274801)
XLA Ops:
  0.6 0.0 copy-start
  0.6 0.8 convert_element_type.52
  1.5 0.8 iota_compare_fusion
  2.3 0.8 copy.24
  3.1 0.8 fusion.22
  3.9 0.0 copy-done
  3.9 0.0 copy-start.1
  3.9 1.0 fusion.30
  4.9 0.2 fusion.9
  5.2 0.6 copy-done.1
  5.8 0.6 fusion.5
  6.4 0.1 broadcast_in_dim.30
  6.5 40.7 %all_to_all.35 = bf16[32,12,1024]{2,1,0:T(8,128)(2,1)} all-to-all(bf16[32,12,1024]{2,1,0:T(8,128)(2,1)S(1)} %broadcast_in_dim.30), channel_id=1, replica_groups=mesh['rep'=16,'head'=8,'pair'=2] {'rep','pair'}, dimensions={0} | all-to-all | bytes 1572864 | tf_op jit(solution)/shard_map/all_to_all | solution.py:13
  47.3 2.1 dot_general.28
  49.4 1.6 fusion.7
  51.0 13.2 %all_to_all.36 = f32[8,48,256]{2,1,0:T(8,128)S(1)} all-to-all(f32[8,48,256]{2,1,0:T(8,128)S(1)} %fusion.7), channel_id=1, replica_groups=mesh['rep'=16,'head'=8,'pair'=2] {'head'}, dimensions={0} | all-to-all | bytes 786432 | tf_op jit(solution)/shard_map/all_to_all | solution.py:35
  64.3 0.6 reduce_sum.46
  64.9 0.8 add_convert_fusion
  65.7 0.0 copy-start.2
  65.7 0.1 broadcast_in_dim.31
  65.8 27.7 %all_to_all.37 = bf16[32,48,256]{2,1,0:T(8,128)(2,1)S(1)} all-to-all(bf16[32,48,256]{2,1,0:T(8,128)(2,1)S(1)} %broadcast_in_dim.31), channel_id=1, replica_groups=mesh['rep'=16,'head'=8,'pair'=2] {'rep','pair'}, dimensions={0} | all-to-all | bytes 1572864 | tf_op jit(solution)/shard_map/all_to_all | solution.py:13
  93.4 0.3 fusion.2
  93.7 0.2 convert_bitcast_fusion
  93.9 0.0 copy-done.2
  93.9 0.0 copy-start.3
  93.9 0.1 copy.23
  94.1 0.6 copy-done.3
  94.7 0.2 multiply_convert_fusion
  94.9 0.0 copy-start.4
  95.0 15.8 %all_to_all.38 = bf16[8,48,1024]{2,1,0:T(8,128)(2,1)S(1)} all-to-all(bf16[8,48,1024]{2,1,0:T(8,128)(2,1)S(1)} %fusion.14), channel_id=1, replica_groups=mesh['rep'=16,'head'=8,'pair'=2] {'head'}, dimensions={0} | all-to-all | bytes 1572864 | tf_op jit(solution)/shard_map/all_to_all | solution.py:104
  110.8 0.0 copy-done.4
  110.8 0.0 copy-start.5
  110.8 1.0 fusion.32
  111.8 0.5 copy-done.5
  112.3 1.0 fusion.31
  113.3 1.7 pad_maximum_fusion
  115.1 3.4 %copy.17 = f32[768,896]{0,1:T(8,128)} copy(f32[768,896]{1,0:T(8,128)} %pad_maximum_fusion) | data formatting | bytes 5505024 | tf_op jit(solution)/shard_map/concatenate | solution.py:40
  118.4 39.0 %all_to_all.39 = f32[8,768,112]{1,2,0:T(8,128)} all-to-all(f32[8,768,112]{1,2,0:T(8,128)} %bitcast.77), channel_id=1, replica_groups=mesh['rep'=16,'head'=8,'pair'=2] {'head'}, dimensions={0} | all-to-all | bytes 5505024 | tf_op jit(solution)/shard_map/all_to_all | solution.py:35
  157.5 2.0 reduce_sum.48
  159.4 0.1 fusion.13
  159.5 0.1 broadcast_in_dim.32
  159.5 15.2 %all_to_all.40 = bf16[8,384,112]{1,2,0:T(8,128)(2,1)} all-to-all(bf16[8,384,112]{1,2,0:T(8,128)(2,1)S(1)} %broadcast_in_dim.32), channel_id=1, replica_groups=mesh['rep'=16,'head'=8,'pair'=2] {'head'}, dimensions={0} | all-to-all | bytes 1376256 | tf_op jit(solution)/shard_map/all_to_all | solution.py:13
  174.8 2.4 %copy.18 = bf16[384,8,112]{2,1,0:T(8,128)(2,1)} copy(bf16[384,8,112]{0,2,1:T(8,128)(2,1)} %bitcast.79) | data formatting | bytes 1376256 | tf_op jit(solution)/shard_map/transpose | solution.py:19
  177.2 2.6 %dot_general.32 = bf16[32,12,896]{2,1,0:T(8,128)(2,1)} reshape(bf16[384,8,112]{2,1,0:T(8,128)(2,1)} %copy.18) | data formatting | bytes 1376256 | tf_op jit(solution)/shard_map/dot_general | solution.py:113
  179.9 2.8 %fusion = f32[32,12,1024]{2,0,1:T(8,128)S(1)} fusion(bf16[896,1024]{1,0:T(8,128)(2,1)} %param.23, bf16[32,12,896]{2,1,0:T(8,128)(2,1)} %dot_general.32), kind=kOutput, calls=%fused_computation.3 | convolution fusion | flops 704643072 | bytes 4096000 | tf_op jit(solution)/shard_map/dot_general | solution.py:113
  182.6 0.9 copy.20
  183.6 56.3 %all_to_all.41 = f32[32,12,1024]{2,1,0:T(8,128)} all-to-all(f32[32,12,1024]{2,1,0:T(8,128)S(1)} %copy.20), channel_id=1, replica_groups=mesh['rep'=16,'head'=8,'pair'=2] {'rep','pair'}, dimensions={0} | all-to-all | bytes 3145728 | tf_op jit(solution)/shard_map/all_to_all | solution.py:35
  239.8 2.3 reduce_sum.49
  (13 shorter events, 0.1 us)
Async XLA Ops:
  0.6 3.3 %copy-start = (bf16[12,1024,128]{2,1,0:T(8,128)(2,1)S(1)}, bf16[12,1024,128]{2,1,0:T(8,128)(2,1)}, u32[]{:S(2)}) copy-start(bf16[12,1024,128]{2,1,0:T(8,128)(2,1)} %param.15) | copy-start | bytes 9437188
  3.9 1.9 copy-start.1
  65.7 28.2 %copy-start.2 = (bf16[48,256]{1,0:T(8,128)(2,1)}, bf16[48,256]{1,0:T(8,128)(2,1)S(1)}, u32[]{:S(2)}) copy-start(bf16[48,256]{1,0:T(8,128)(2,1)S(1)} %add_convert_fusion) | copy-start | bytes 73732
  93.9 0.8 copy-start.3
  94.9 15.9 %copy-start.4 = (bf16[1024,896]{1,0:T(8,128)(2,1)S(1)}, bf16[1024,896]{1,0:T(8,128)(2,1)}, u32[]{:S(2)}) copy-start(bf16[1024,896]{1,0:T(8,128)(2,1)} %param.22) | copy-start | bytes 5505028
  110.8 1.5 copy-start.5
